TPU v7x, 32 devices: a whole 2x2x4 slice. The times are simulated.
32 devices in a mesh: groups: 2 (over y), tmpl: 16 (over z, x, core).
Axes of the slice: x: 2, y: 2, z: 4, core: 2. Of those that a mesh axis runs over, the one named last changes fastest.
Arguments:
- records: bfloat16 [512, 3, 768], P(('groups', 'tmpl')), parts along dimension 0, may hold values from -200 to 200, as said below
- templates: bfloat16 [96, 20, 3, 300], P('tmpl'), may hold values from -6 to 6
- fetch_list: int32 [16, 16, 2], P('tmpl'), may hold values from -1 to 15, as said below
- cluster_slots: int32 [96, 20], P('tmpl'), may hold values from 0 to 31, as said below
- moveouts: int32 [96, 20], P('tmpl'), may hold values from 0 to 213
Outputs:
- stack: float32 [192, 256], P(('groups', 'tmpl')), parts along dimension 0
- network_peak: float32 [512], P('groups'), parts along dimension 0
There are 2 independent parts, one for each index of `groups`. A program takes and returns all parts, laid end to end along the dimension named above; an argument that names none is the same for every part. Nothing has to cross between parts.
Inputs may be any that keep to these rules, and one draw needn't show every extreme that they name: Values are the records' samples; the amplitude of a station component is steady apart from one event burst. fetch_list[g, o, s] is an index among holder o's 16 stations, or -1 for an empty slot; the set entries of one (g, o) pair differ; every group g has all 2 slots set for the holders g to g + 20 // 2 - 1 (modulo 16). cluster_slots[k, j] is a slot o * 2 + s of group k // 6 whose fetch_list entry is set; the 20 entries of a station set differ, and every set slot of a group is named by some station set of that group.
All inputs are finite; a program needn't handle non-finite values.
Results may differ from a plain program's by a relative error of at most 0.0003.
Values may be sent and summed in bfloat16 or wider, within the bound.
A program may use at most 64 MiB of HBM per device.

v0:
```python
import jax
import jax.numpy as jnp
from jax import lax
from jax.sharding import PartitionSpec as P

OUT = 256


def batch_stack(traces, kernels, shifts):
    sets_here, stations, comps, rec_len = traces.shape
    members = kernels.shape[1]
    tap_count = kernels.shape[-1]
    lag_count = rec_len - tap_count + 1
    inputs_nch = traces.reshape(1, sets_here * stations * comps, rec_len)
    filters = jnp.transpose(kernels, (0, 2, 3, 1, 4)).reshape(
        sets_here * stations * comps * members, 1, tap_count
    )
    products = lax.conv_general_dilated(
        inputs_nch,
        filters,
        (1,),
        "VALID",
        dimension_numbers=("NCH", "OIH", "NCH"),
        feature_group_count=sets_here * stations * comps,
        preferred_element_type=jnp.float32,
    )[0]
    products = products.reshape(sets_here, stations, comps, members, lag_count)
    widened = traces.astype(jnp.float32)
    running = jnp.cumsum(widened * widened, axis=-1)
    running = jnp.concatenate(
        [jnp.zeros((sets_here, stations, comps, 1), jnp.float32), running], axis=-1
    )
    energy = running[..., tap_count:] - running[..., :lag_count]
    data_scale = jnp.sqrt(energy / tap_count + 1e-05)
    kernels_wide = kernels.astype(jnp.float32)
    tmpl_scale = jnp.sqrt(jnp.mean(kernels_wide * kernels_wide, axis=-1) + 1e-05)
    tmpl_scale = jnp.transpose(tmpl_scale, (0, 2, 3, 1))[..., None]
    normed = products / (tap_count * tmpl_scale * data_scale[:, :, :, None, :])
    channel_sum = jnp.sum(normed, axis=2)
    offsets = jnp.transpose(shifts, (0, 2, 1))[..., None] + jnp.arange(OUT, dtype=jnp.int32)
    aligned = jnp.take_along_axis(channel_sum, offsets, axis=3)
    return jnp.sum(aligned, axis=1)


def on_device(records, templates, fetch_list, cluster_slots, moveouts):
    owners = lax.axis_size("tmpl")
    per_owner = fetch_list.shape[2]
    stations_here = records.shape[0]
    slot_total = owners * per_owner
    wanted = fetch_list.reshape(slot_total)
    block_rows = lax.all_gather(records, "tmpl", axis=0, tiled=True)
    owners_in = block_rows.shape[0] // stations_here
    row_ids = jnp.arange(
        owners_in * per_owner, dtype=jnp.int32
    ) // per_owner * stations_here + jnp.clip(wanted, 0, stations_here - 1)
    rows_taken = jnp.take(block_rows, row_ids, axis=0)
    rows_taken = jnp.where(
        (wanted >= 0)[:, None, None], rows_taken, jnp.zeros((), block_rows.dtype)
    )
    clusters_here = cluster_slots.shape[0]
    members = templates.shape[0] // clusters_here
    kernels_all = templates.reshape((clusters_here, members) + templates.shape[1:])
    shifts_all = moveouts.reshape(clusters_here, members, moveouts.shape[1])
    traces = jnp.take(rows_taken, cluster_slots, axis=0)
    stacks = batch_stack(traces, kernels_all, shifts_all)
    stack = stacks.reshape(clusters_here * members, stacks.shape[-1])
    network_peak = lax.pmax(jnp.max(stack, axis=0), "tmpl")
    return (stack, network_peak)


def solution(mesh):
    placed = (
        P(("groups", "tmpl"), None, None),
        P("tmpl", None, None, None),
        P("tmpl", None, None),
        P("tmpl", None),
        P("tmpl", None),
    )
    return jax.shard_map(
        on_device,
        mesh=mesh,
        in_specs=placed,
        out_specs=(P(("groups", "tmpl"), None), P("groups")),
        check_vma=False,
    )
```

profile of v0, /device:TPU:0, one launch (start us, length us, event | category | flops | bytes accessed | tf_op | source)
XLA Modules:
  0.0 464.8 jit_solution(15089831089222544754)
XLA Ops:
  7.2 0.7 all-gather.2.cloned.1.call-update
  7.9 0.7 broadcast_clamp_fusion
  8.9 0.7 broadcast_compare_fusion
  9.8 0.7 compare_select_fusion.2
  10.5 0.7 compare_and_fusion
  11.3 0.2 broadcast_in_dim.53
  11.5 1.1 copy.62
  12.7 0.2 reshape_transpose_reshape.3
  12.9 1.3 copy.64
  14.8 36.6 %all-gather.2.cloned.1.call-done = bf16[256,3,768]{2,0,1:T(8,128)(2,1)} async-done(((bf16[16,3,768]{2,0,1:T(8,128)(2,1)}), bf16[256,3,768]{2,0,1:T(8,128)(2,1)}) %all-gather.2.cloned.1.call-update) | async-done | bytes 1179664 | tf_op jit(solution)/shard_map/all_gather | solution.py:51
  51.4 2.3 copy.61
  53.7 0.7 gather_fusion
  54.4 0.2 select_select_fusion
  54.6 1.2 gather_fusion.1
  55.8 0.5 reshape.256
  56.4 1.3 gather.18
  57.6 0.2 convert_multiply_fusion
  57.9 30.9 %reduce-window.6 = f32[6,20,3,6,128]{4,1,2,3,0:T(8,128)S(1)} reduce-window(f32[6,20,3,6,128]{4,1,2,3,0:T(8,128)S(1)} %copy.70, f32[]{:T(128)} %constant.84.clone.1), window={size=1x1x1x1x128 pad=0_0x0_0x0_0x0_0x127_0}, to_apply=%region_1.2 | reduce-window | flops 35112960 | bytes 2211844 | tf_op jit(solution)/shard_map/reduce-window
  88.9 0.4 slice.23
  89.3 1.0 copy.71
  90.4 0.5 broadcast_add_fusion
  90.8 0.3 copy.78
  91.1 0.6 reshape.257
  91.7 1.2 broadcast_select_fusion
  92.8 1.3 copy.63
  94.2 25.0 %fusion.19 = f32[1,360,469]{1,0,2:T(1,128)} fusion(bf16[1,360,768]{1,0,2:T(2,128)(2,1)S(1)} %copy.63, bf16[360,1,300]{0,1,2:T(2,128)(2,1)} %copy.64), kind=kOutput, calls=%fused_computation.50 | convolution fusion | flops 101304000 | bytes 1444320 | tf_op jit(solution)/shard_map/conv_general_dilated | solution.py:18
  119.1 2.3 copy.65
  121.4 0.3 reshape_squeeze.3
  121.8 2.3 fusion.6
  124.1 301.2 %gather_fusion.2 = f32[30720]{0:T(1024)S(1)} fusion(f32[6,20,469]{2,1,0:T(8,128)S(1)} %fusion.6, s32[30720]{0:T(1024)S(1)} %reshape.244), kind=kCustom, calls=%fused_computation.2 | custom fusion | bytes 614400 | tf_op jit(solution)/shard_map/jit(take_along_axis)/gather | solution.py:41
  425.3 0.4 fusion.10
  425.7 32.2 %pmax.7 = f32[256]{0:T(256)} all-reduce(f32[256]{0:T(256)S(1)} %reduce_max.9), channel_id=1, replica_groups=mesh['groups'=2,'tmpl'=16] {'tmpl'}, use_global_device_ids=true, to_apply=%region_6.7 | all-reduce | flops 256 | bytes 2048 | tf_op jit(solution)/shard_map/pmax | solution.py:67
  (27 shorter events, 1.3 us)
Async XLA Ops:
  7.2 7.1 %copy-start = (bf16[6,20,3,300]{3,1,2,0:T(8,128)(2,1)S(1)}, bf16[6,20,3,300]{3,1,2,0:T(8,128)(2,1)}, u32[]{:S(2)}) copy-start(bf16[6,20,3,300]{3,1,2,0:T(8,128)(2,1)} %param.6) | copy-start | bytes 648004
  7.2 7.4 %copy-start.2 = (s32[6,20]{1,0:T(8,128)S(1)}, s32[6,20]{1,0:T(8,128)}, u32[]{:S(2)}) copy-start(s32[6,20]{1,0:T(8,128)} %param.9) | copy-start | bytes 1444
  7.2 44.2 %all-gather.2.cloned.1.call-start = ((), (), s32[]{:S(2)}) async-start(), calls=%async_computation | async-start | bytes 1253376 | tf_op jit(solution)/shard_map/all_gather | solution.py:51
  425.7 32.2 %copy-start.1 = (f32[6,256]{1,0:T(8,128)}, f32[6,256]{1,0:T(8,128)S(1)}, u32[]{:S(2)}) copy-start(f32[6,256]{1,0:T(8,128)S(1)} %fusion.10) | copy-start | bytes 18436
Sparse Core Ops, SparseCore 0:
  10.3 41.0 all-gather.1
where the time goes:
time: 465 us
  local copies, waits for them, and re-layouts  317 us (68%)
  other arithmetic  38.9 us (8%)
  waiting for transfers between devices  37.3 us (8%)
  blocking collectives  32.2 us (7%)
  matrix products  25 us (5%)
  between operations  14.3 us (3%)
    gather x2, local copies, waits for them, and re-layouts, batch_stack(): aligned = jnp.take_along_axis(channel_sum, offsets, axis=3)  301 us
    all_gather x1, waiting for transfers between devices, on_device(): block_rows = lax.all_gather(records, 'tmpl', axis=0, tiled=True)  36.6 us
    pmax x1, blocking collectives, on_device(): network_peak = lax.pmax(jnp.max(stack, axis=0), 'tmpl')  32.2 us
    another operation x3, other arithmetic  31.5 us
    conv_general_dilated x1, matrix products, batch_stack(): lax.conv_general_dilated(inputs_nch, filters, (1,), 'VALID', dimension_nu...  25 us
  transfers between devices with their start and end apart: 1, of which 1 were waited for; matrix products, arithmetic and copies ran while one was open for 1% of the time, Pallas kernels for 0%

commit v1 on v0

--- a/solution.py
+++ b/solution.py
@@ -48,7 +48,12 @@
     stations_here = records.shape[0]
     slot_total = owners * per_owner
     wanted = fetch_list.reshape(slot_total)
-    block_rows = lax.all_gather(records, "tmpl", axis=0, tiled=True)
+    ring = [records]
+    for hop in range(15):
+        ring.append(lax.ppermute(ring[-1], "tmpl", [(dev, (dev + 1) % 16) for dev in range(16)]))
+    block_rows = jnp.roll(
+        jnp.concatenate(ring[::-1], axis=0), (lax.axis_index("tmpl") + 1) * ring[0].shape[0], axis=0
+    )
     owners_in = block_rows.shape[0] // stations_here
     row_ids = jnp.arange(
         owners_in * per_owner, dtype=jnp.int32

time: 465 us -> 509 us (1.095)
  waiting for transfers between devices: 37.3 us -> 93.1 us
  between operations: 14.3 us -> 1.07 us
    ppermute x0 -> x15, waiting for transfers between devices: none -> 93.1 us  [on_device(): lax.ppermute(ring[-1], 'tmpl', [(dev, (dev + 1) % 16) for dev in range(16)])]
    all_gather x1 -> x0, waiting for transfers between devices: 36.6 us -> none  [on_device(): block_rows = lax.all_gather(records, 'tmpl', axis=0, tiled=True)]
  transfers between devices with their start and end apart: 1 -> 15, of which waited for: 1 -> 15; matrix products, arithmetic and copies ran while one was open for 1% -> 2% of each run, Pallas kernels for 0% -> 0%
where the time goes in v1:
time: 509 us; the launch traced here: 508 us
  local copies, waits for them, and re-layouts  318 us (62%)
  waiting for transfers between devices  93.1 us (18%)
  other arithmetic  40.4 us (8%)
  blocking collectives  30 us (6%)
  matrix products  24.8 us (5%)
    gather x2, local copies, waits for them, and re-layouts, batch_stack(): aligned = jnp.take_along_axis(channel_sum, offsets, axis=3)  301 us
    ppermute x15, waiting for transfers between devices, on_device(): lax.ppermute(ring[-1], 'tmpl', [(dev, (dev + 1) % 16) for dev in range(16)])  93.1 us
    another operation x3, other arithmetic  31.4 us
    pmax x1, blocking collectives, on_device(): network_peak = lax.pmax(jnp.max(stack, axis=0), 'tmpl')  30 us
    conv_general_dilated x1, matrix products, batch_stack(): lax.conv_general_dilated(inputs_nch, filters, (1,), 'VALID', dimension_nu...  24.8 us
  transfers between devices with their start and end apart: 15, of which 15 were waited for; matrix products, arithmetic and copies ran while one was open for 2% of the time, Pallas kernels for 0%

profile of v1, /device:TPU:0, one launch (start us, length us, event | category | flops | bytes accessed | tf_op | source)
XLA Modules:
  0.0 508.3 jit_solution(12030554645026508508)
XLA Ops:
  0.6 1.0 copy.66
  2.1 7.3 %collective-permute-done = bf16[16,3,768]{2,1,0:T(4,128)(2,1)S(1)} collective-permute-done((bf16[16,3,768]{2,1,0:T(4,128)(2,1)S(1)}, bf16[16,3,768]{2,1,0:T(4,128)(2,1)S(1)}, u32[]{:S(2)}, u32[]{:S(2)}) %collective-permute-start) | collective-permute-done | bytes 73760 | tf_op jit(solution)/shard_map/ppermute | solution.py:53
  9.4 6.7 %collective-permute-done.1 = bf16[16,3,768]{2,1,0:T(4,128)(2,1)S(1)} collective-permute-done((bf16[16,3,768]{2,1,0:T(4,128)(2,1)S(1)}, bf16[16,3,768]{2,1,0:T(4,128)(2,1)S(1)}, u32[]{:S(2)}, u32[]{:S(2)}) %collective-permute-start.1) | collective-permute-done | bytes 73760 | tf_op jit(solution)/shard_map/ppermute | solution.py:53
  16.2 6.7 %collective-permute-done.2 = bf16[16,3,768]{2,1,0:T(4,128)(2,1)S(1)} collective-permute-done((bf16[16,3,768]{2,1,0:T(4,128)(2,1)S(1)}, bf16[16,3,768]{2,1,0:T(4,128)(2,1)S(1)}, u32[]{:S(2)}, u32[]{:S(2)}) %collective-permute-start.2) | collective-permute-done | bytes 73760 | tf_op jit(solution)/shard_map/ppermute | solution.py:53
  22.9 6.7 %collective-permute-done.3 = bf16[16,3,768]{2,1,0:T(4,128)(2,1)S(1)} collective-permute-done((bf16[16,3,768]{2,1,0:T(4,128)(2,1)S(1)}, bf16[16,3,768]{2,1,0:T(4,128)(2,1)S(1)}, u32[]{:S(2)}, u32[]{:S(2)}) %collective-permute-start.3) | collective-permute-done | bytes 73760 | tf_op jit(solution)/shard_map/ppermute | solution.py:53
  29.6 6.7 %collective-permute-done.4 = bf16[16,3,768]{2,1,0:T(4,128)(2,1)S(1)} collective-permute-done((bf16[16,3,768]{2,1,0:T(4,128)(2,1)S(1)}, bf16[16,3,768]{2,1,0:T(4,128)(2,1)S(1)}, u32[]{:S(2)}, u32[]{:S(2)}) %collective-permute-start.4) | collective-permute-done | bytes 73760 | tf_op jit(solution)/shard_map/ppermute | solution.py:53
  36.4 0.8 fusion.9
  37.2 5.9 %collective-permute-done.5 = bf16[16,3,768]{2,1,0:T(4,128)(2,1)S(1)} collective-permute-done((bf16[16,3,768]{2,1,0:T(4,128)(2,1)S(1)}, bf16[16,3,768]{2,1,0:T(4,128)(2,1)S(1)}, u32[]{:S(2)}, u32[]{:S(2)}) %collective-permute-start.5) | collective-permute-done | bytes 73760 | tf_op jit(solution)/shard_map/ppermute | solution.py:53
  43.1 1.1 multiply_reduce_fusion
  44.2 5.6 %collective-permute-done.6 = bf16[16,3,768]{2,1,0:T(4,128)(2,1)S(1)} collective-permute-done((bf16[16,3,768]{2,1,0:T(4,128)(2,1)S(1)}, bf16[16,3,768]{2,1,0:T(4,128)(2,1)S(1)}, u32[]{:S(2)}, u32[]{:S(2)}) %collective-permute-start.6) | collective-permute-done | bytes 73760 | tf_op jit(solution)/shard_map/ppermute | solution.py:53
  49.9 6.7 %collective-permute-done.7 = bf16[16,3,768]{2,1,0:T(4,128)(2,1)S(1)} collective-permute-done((bf16[16,3,768]{2,1,0:T(4,128)(2,1)S(1)}, bf16[16,3,768]{2,1,0:T(4,128)(2,1)S(1)}, u32[]{:S(2)}, u32[]{:S(2)}) %collective-permute-start.7) | collective-permute-done | bytes 73760 | tf_op jit(solution)/shard_map/ppermute | solution.py:53
  57.3 6.0 %collective-permute-done.8 = bf16[16,3,768]{2,1,0:T(4,128)(2,1)S(1)} collective-permute-done((bf16[16,3,768]{2,1,0:T(4,128)(2,1)S(1)}, bf16[16,3,768]{2,1,0:T(4,128)(2,1)S(1)}, u32[]{:S(2)}, u32[]{:S(2)}) %collective-permute-start.8) | collective-permute-done | bytes 73760 | tf_op jit(solution)/shard_map/ppermute | solution.py:53
  64.0 6.0 %collective-permute-done.9 = bf16[16,3,768]{2,1,0:T(4,128)(2,1)S(1)} collective-permute-done((bf16[16,3,768]{2,1,0:T(4,128)(2,1)S(1)}, bf16[16,3,768]{2,1,0:T(4,128)(2,1)S(1)}, u32[]{:S(2)}, u32[]{:S(2)}) %collective-permute-start.9) | collective-permute-done | bytes 73760 | tf_op jit(solution)/shard_map/ppermute | solution.py:53
  70.8 6.1 %collective-permute-done.10 = bf16[16,3,768]{2,1,0:T(4,128)(2,1)S(1)} collective-permute-done((bf16[16,3,768]{2,1,0:T(4,128)(2,1)S(1)}, bf16[16,3,768]{2,1,0:T(4,128)(2,1)S(1)}, u32[]{:S(2)}, u32[]{:S(2)}) %collective-permute-start.10) | collective-permute-done | bytes 73760 | tf_op jit(solution)/shard_map/ppermute | solution.py:53
  77.7 5.9 %collective-permute-done.11 = bf16[16,3,768]{2,1,0:T(4,128)(2,1)S(1)} collective-permute-done((bf16[16,3,768]{2,1,0:T(4,128)(2,1)S(1)}, bf16[16,3,768]{2,1,0:T(4,128)(2,1)S(1)}, u32[]{:S(2)}, u32[]{:S(2)}) %collective-permute-start.11) | collective-permute-done | bytes 73760 | tf_op jit(solution)/shard_map/ppermute | solution.py:53
  83.6 6.6 %collective-permute-done.12 = bf16[16,3,768]{2,1,0:T(4,128)(2,1)S(1)} collective-permute-done((bf16[16,3,768]{2,1,0:T(4,128)(2,1)S(1)}, bf16[16,3,768]{2,1,0:T(4,128)(2,1)S(1)}, u32[]{:S(2)}, u32[]{:S(2)}) %collective-permute-start.12) | collective-permute-done | bytes 73760 | tf_op jit(solution)/shard_map/ppermute | solution.py:53
  90.3 1.1 copy.70
  92.3 1.3 copy.72
  93.8 3.3 collective-permute-done.13
  97.0 6.7 %collective-permute-done.14 = bf16[16,3,768]{2,1,0:T(4,128)(2,1)S(1)} collective-permute-done((bf16[16,3,768]{2,1,0:T(4,128)(2,1)S(1)}, bf16[16,3,768]{2,1,0:T(4,128)(2,1)S(1)}, u32[]{:S(2)}, u32[]{:S(2)}) %collective-permute-start.14) | collective-permute-done | bytes 73760 | tf_op jit(solution)/shard_map/ppermute | solution.py:53
  106.1 0.7 gather_fusion
  107.0 1.2 gather_fusion.1
  109.0 1.3 gather.18
  110.5 30.9 %reduce-window.6 = f32[6,20,3,6,128]{4,1,2,3,0:T(8,128)S(1)} reduce-window(f32[6,20,3,6,128]{4,1,2,3,0:T(8,128)S(1)} %copy.78, f32[]{:T(128)} %constant.109.clone.1), window={size=1x1x1x1x128 pad=0_0x0_0x0_0x0_0x127_0}, to_apply=%region_1.2 | reduce-window | flops 35112960 | bytes 2211844 | tf_op jit(solution)/shard_map/reduce-window
  141.9 0.9 copy.79
  144.2 1.2 broadcast_select_fusion
  145.4 1.3 copy.71
  146.7 24.8 %fusion.19 = f32[1,360,469]{1,0,2:T(1,128)} fusion(bf16[1,360,768]{1,0,2:T(2,128)(2,1)S(1)} %copy.71, bf16[360,1,300]{0,1,2:T(2,128)(2,1)} %copy.72), kind=kOutput, calls=%fused_computation.83 | convolution fusion | flops 101304000 | bytes 1444320 | tf_op jit(solution)/shard_map/conv_general_dilated | solution.py:18
  171.5 2.5 copy.73
  174.4 2.3 fusion.6
  176.6 301.2 %gather_fusion.2 = f32[30720]{0:T(1024)S(1)} fusion(f32[6,20,469]{2,1,0:T(8,128)S(1)} %fusion.6, s32[30720]{0:T(1024)S(1)} %reshape.244), kind=kCustom, calls=%fused_computation.2 | custom fusion | bytes 614400 | tf_op jit(solution)/shard_map/jit(take_along_axis)/gather | solution.py:41
  478.2 30.0 %pmax.7 = f32[256]{0:T(256)} all-reduce(f32[256]{0:T(256)S(1)} %reduce_max.9), channel_id=1, replica_groups=mesh['groups'=2,'tmpl'=16] {'tmpl'}, use_global_device_ids=true, to_apply=%region_6.7 | all-reduce | flops 256 | bytes 2048 | tf_op jit(solution)/shard_map/pmax | solution.py:72
  (86 shorter events, 10.4 us)
Async XLA Ops:
  0.6 103.9 %copy-start = (bf16[16,3,768]{2,0,1:T(8,128)(2,1)S(1)}, bf16[16,3,768]{2,0,1:T(8,128)(2,1)}, u32[]{:S(2)}) copy-start(bf16[16,3,768]{2,0,1:T(8,128)(2,1)} %param.5) | copy-start | bytes 221188
  1.6 7.8 %collective-permute-start = (bf16[16,3,768]{2,1,0:T(4,128)(2,1)S(1)}, bf16[16,3,768]{2,1,0:T(4,128)(2,1)S(1)}, u32[]{:S(2)}, u32[]{:S(2)}) collective-permute-start(bf16[16,3,768]{2,1,0:T(4,128)(2,1)S(1)} %copy.66), channel_id=1, source_target_pairs={{0,1},{1,2},{2,3},{3,4},{4,5},{5,6},{6,7},{7,8},{8,9},{9,10},{10,1... | collective-permute-start | bytes 221192 | tf_op jit(solution)/shard_map/ppermute | solution.py:53
  9.4 6.7 %collective-permute-start.1 = (bf16[16,3,768]{2,1,0:T(4,128)(2,1)S(1)}, bf16[16,3,768]{2,1,0:T(4,128)(2,1)S(1)}, u32[]{:S(2)}, u32[]{:S(2)}) collective-permute-start(bf16[16,3,768]{2,1,0:T(4,128)(2,1)S(1)} %collective-permute-done), channel_id=1, source_target_pairs={{0,1},{1,2},{2,3},{3,4},{4,5},{5,6},{6,7},{7,8},{8,9},{9,10},{10,1... | collective-permute-start | bytes 221192 | tf_op jit(solution)/shard_map/ppermute | solution.py:53
  16.2 6.7 %collective-permute-start.2 = (bf16[16,3,768]{2,1,0:T(4,128)(2,1)S(1)}, bf16[16,3,768]{2,1,0:T(4,128)(2,1)S(1)}, u32[]{:S(2)}, u32[]{:S(2)}) collective-permute-start(bf16[16,3,768]{2,1,0:T(4,128)(2,1)S(1)} %collective-permute-done.1), channel_id=1, source_target_pairs={{0,1},{1,2},{2,3},{3,4},{4,5},{5,6},{6,7},{7,8},{8,9},{9,10},{10,1... | collective-permute-start | bytes 221192 | tf_op jit(solution)/shard_map/ppermute | solution.py:53
  22.9 6.7 %collective-permute-start.3 = (bf16[16,3,768]{2,1,0:T(4,128)(2,1)S(1)}, bf16[16,3,768]{2,1,0:T(4,128)(2,1)S(1)}, u32[]{:S(2)}, u32[]{:S(2)}) collective-permute-start(bf16[16,3,768]{2,1,0:T(4,128)(2,1)S(1)} %collective-permute-done.2), channel_id=1, source_target_pairs={{0,1},{1,2},{2,3},{3,4},{4,5},{5,6},{6,7},{7,8},{8,9},{9,10},{10,1... | collective-permute-start | bytes 221192 | tf_op jit(solution)/shard_map/ppermute | solution.py:53
  29.6 6.7 %collective-permute-start.4 = (bf16[16,3,768]{2,1,0:T(4,128)(2,1)S(1)}, bf16[16,3,768]{2,1,0:T(4,128)(2,1)S(1)}, u32[]{:S(2)}, u32[]{:S(2)}) collective-permute-start(bf16[16,3,768]{2,1,0:T(4,128)(2,1)S(1)} %collective-permute-done.3), channel_id=1, source_target_pairs={{0,1},{1,2},{2,3},{3,4},{4,5},{5,6},{6,7},{7,8},{8,9},{9,10},{10,1... | collective-permute-start | bytes 221192 | tf_op jit(solution)/shard_map/ppermute | solution.py:53
  36.4 6.7 %collective-permute-start.5 = (bf16[16,3,768]{2,1,0:T(4,128)(2,1)S(1)}, bf16[16,3,768]{2,1,0:T(4,128)(2,1)S(1)}, u32[]{:S(2)}, u32[]{:S(2)}) collective-permute-start(bf16[16,3,768]{2,1,0:T(4,128)(2,1)S(1)} %collective-permute-done.4), channel_id=1, source_target_pairs={{0,1},{1,2},{2,3},{3,4},{4,5},{5,6},{6,7},{7,8},{8,9},{9,10},{10,1... | collective-permute-start | bytes 221192 | tf_op jit(solution)/shard_map/ppermute | solution.py:53
  43.1 6.7 %collective-permute-start.6 = (bf16[16,3,768]{2,1,0:T(4,128)(2,1)S(1)}, bf16[16,3,768]{2,1,0:T(4,128)(2,1)S(1)}, u32[]{:S(2)}, u32[]{:S(2)}) collective-permute-start(bf16[16,3,768]{2,1,0:T(4,128)(2,1)S(1)} %collective-permute-done.5), channel_id=1, source_target_pairs={{0,1},{1,2},{2,3},{3,4},{4,5},{5,6},{6,7},{7,8},{8,9},{9,10},{10,1... | collective-permute-start | bytes 221192 | tf_op jit(solution)/shard_map/ppermute | solution.py:53
  49.8 6.7 %collective-permute-start.7 = (bf16[16,3,768]{2,1,0:T(4,128)(2,1)S(1)}, bf16[16,3,768]{2,1,0:T(4,128)(2,1)S(1)}, u32[]{:S(2)}, u32[]{:S(2)}) collective-permute-start(bf16[16,3,768]{2,1,0:T(4,128)(2,1)S(1)} %collective-permute-done.6), channel_id=1, source_target_pairs={{0,1},{1,2},{2,3},{3,4},{4,5},{5,6},{6,7},{7,8},{8,9},{9,10},{10,1... | collective-permute-start | bytes 221192 | tf_op jit(solution)/shard_map/ppermute | solution.py:53
  56.6 6.7 %collective-permute-start.8 = (bf16[16,3,768]{2,1,0:T(4,128)(2,1)S(1)}, bf16[16,3,768]{2,1,0:T(4,128)(2,1)S(1)}, u32[]{:S(2)}, u32[]{:S(2)}) collective-permute-start(bf16[16,3,768]{2,1,0:T(4,128)(2,1)S(1)} %collective-permute-done.7), channel_id=1, source_target_pairs={{0,1},{1,2},{2,3},{3,4},{4,5},{5,6},{6,7},{7,8},{8,9},{9,10},{10,1... | collective-permute-start | bytes 221192 | tf_op jit(solution)/shard_map/ppermute | solution.py:53
  63.3 6.7 %collective-permute-start.9 = (bf16[16,3,768]{2,1,0:T(4,128)(2,1)S(1)}, bf16[16,3,768]{2,1,0:T(4,128)(2,1)S(1)}, u32[]{:S(2)}, u32[]{:S(2)}) collective-permute-start(bf16[16,3,768]{2,1,0:T(4,128)(2,1)S(1)} %collective-permute-done.8), channel_id=1, source_target_pairs={{0,1},{1,2},{2,3},{3,4},{4,5},{5,6},{6,7},{7,8},{8,9},{9,10},{10,1... | collective-permute-start | bytes 221192 | tf_op jit(solution)/shard_map/ppermute | solution.py:53
  70.1 6.7 %collective-permute-start.10 = (bf16[16,3,768]{2,1,0:T(4,128)(2,1)S(1)}, bf16[16,3,768]{2,1,0:T(4,128)(2,1)S(1)}, u32[]{:S(2)}, u32[]{:S(2)}) collective-permute-start(bf16[16,3,768]{2,1,0:T(4,128)(2,1)S(1)} %collective-permute-done.9), channel_id=1, source_target_pairs={{0,1},{1,2},{2,3},{3,4},{4,5},{5,6},{6,7},{7,8},{8,9},{9,10},{10,1... | collective-permute-start | bytes 221192 | tf_op jit(solution)/shard_map/ppermute | solution.py:53
  76.8 6.7 %collective-permute-start.11 = (bf16[16,3,768]{2,1,0:T(4,128)(2,1)S(1)}, bf16[16,3,768]{2,1,0:T(4,128)(2,1)S(1)}, u32[]{:S(2)}, u32[]{:S(2)}) collective-permute-start(bf16[16,3,768]{2,1,0:T(4,128)(2,1)S(1)} %collective-permute-done.10), channel_id=1, source_target_pairs={{0,1},{1,2},{2,3},{3,4},{4,5},{5,6},{6,7},{7,8},{8,9},{9,10},{10,1... | collective-permute-start | bytes 221192 | tf_op jit(solution)/shard_map/ppermute | solution.py:53
  83.5 6.7 %collective-permute-start.12 = (bf16[16,3,768]{2,1,0:T(4,128)(2,1)S(1)}, bf16[16,3,768]{2,1,0:T(4,128)(2,1)S(1)}, u32[]{:S(2)}, u32[]{:S(2)}) collective-permute-start(bf16[16,3,768]{2,1,0:T(4,128)(2,1)S(1)} %collective-permute-done.11), channel_id=1, source_target_pairs={{0,1},{1,2},{2,3},{3,4},{4,5},{5,6},{6,7},{7,8},{8,9},{9,10},{10,1... | collective-permute-start | bytes 221192 | tf_op jit(solution)/shard_map/ppermute | solution.py:53
  90.3 6.7 %collective-permute-start.13 = (bf16[16,3,768]{2,1,0:T(4,128)(2,1)S(1)}, bf16[16,3,768]{2,1,0:T(4,128)(2,1)S(1)}, u32[]{:S(2)}, u32[]{:S(2)}) collective-permute-start(bf16[16,3,768]{2,1,0:T(4,128)(2,1)S(1)} %collective-permute-done.12), channel_id=1, source_target_pairs={{0,1},{1,2},{2,3},{3,4},{4,5},{5,6},{6,7},{7,8},{8,9},{9,10},{10,1... | collective-permute-start | bytes 221192 | tf_op jit(solution)/shard_map/ppermute | solution.py:53
  97.0 6.7 %collective-permute-start.14 = (bf16[16,3,768]{2,1,0:T(4,128)(2,1)S(1)}, bf16[16,3,768]{2,1,0:T(4,128)(2,1)S(1)}, u32[]{:S(2)}, u32[]{:S(2)}) collective-permute-start(bf16[16,3,768]{2,1,0:T(4,128)(2,1)S(1)} %collective-permute-done.13), channel_id=1, source_target_pairs={{0,1},{1,2},{2,3},{3,4},{4,5},{5,6},{6,7},{7,8},{8,9},{9,10},{10,1... | collective-permute-start | bytes 221192 | tf_op jit(solution)/shard_map/ppermute | solution.py:53
  176.6 301.2 %copy-start.2 = (s32[6,20]{1,0:T(8,128)S(1)}, s32[6,20]{1,0:T(8,128)}, u32[]{:S(2)}) copy-start(s32[6,20]{1,0:T(8,128)} %param.9) | copy-start | bytes 1444
  478.2 30.1 %copy-start.1 = (f32[6,256]{1,0:T(8,128)}, f32[6,256]{1,0:T(8,128)S(1)}, u32[]{:S(2)}) copy-start(f32[6,256]{1,0:T(8,128)S(1)} %fusion.10) | copy-start | bytes 18436
